TPU v7x, 256 devices: a whole 4x4x8 slice. The times are simulated.
256 devices in a mesh: fsdp: 8 (over z_hi, y), tensor: 32 (over x, z_lo, core).
Axes of the slice: x: 4, y: 4, z: 8 (z_hi: 2, z_lo: 4; z = z_hi * 4 + z_lo), core: 2. Of those that a mesh axis runs over, the one named last changes fastest.
Arguments:
- momentum: bfloat16 [8192, 28672], P('fsdp', 'tensor'), may hold values from -6 to 6
- gradient: bfloat16 [8192, 28672], P('fsdp', 'tensor'), may hold values from -4 to 4
- factor: float32 [28672, 512], P('tensor', 'fsdp'), may hold values from -0.03125 to 0.03125
Outputs:
- new_momentum: bfloat16 [8192, 28672], P('fsdp', 'tensor')
- new_factor: float32 [28672, 512], P('tensor', 'fsdp')
- update: bfloat16 [8192, 28672], P('fsdp', 'tensor')
All inputs are finite; a program needn't handle non-finite values.
Results may differ from a plain program's by a relative error of at most 0.017.
Values may be sent and summed in bfloat16 or wider, within the bound.
No kernel may reach another device: no remote copies, remote signals or barrier semaphores. Data moves between devices by JAX's collectives and lax.ppermute only.
A program may use at most 64 MiB of HBM per device.

v0:
```python
import jax
import jax.numpy as jnp
from jax import lax
from jax.experimental import pallas as pl
from jax.experimental.pallas import tpu as pltpu
from jax.sharding import Mesh
from jax.sharding import PartitionSpec as P

D = 8192
FF = 28672
R = 512
FAR = 16
BLOCK = 128
BLOCKS = R // BLOCK
PAIRS = [(i, j) for i in range(BLOCKS) for j in range(i + 1)]
SHARE = len(PAIRS) * BLOCK // (2 * FAR)
SUB = 8
TENSOR = ("x", "z_lo", "core")

decay_rate = 0.95
epsilon = 1e-06
f32 = jnp.float32
bf16 = jnp.bfloat16


def product(left, right, left_dim, right_dim):
    return lax.dot_general(left, right, (((left_dim,), (right_dim,)), ((), ())), preferred_element_type=f32)


def added(terms):
    while len(terms) > 1:
        terms = [
            terms[i] + terms[i + 1] if i + 1 < len(terms) else terms[i] for i in range(0, len(terms), 2)
        ]
    return terms[0]


def spread(value):
    return jnp.broadcast_to(value, (SUB, BLOCK))


def small_inverse(entries):
    rest = [row[:] for row in entries]
    inverse = [None] * SUB
    upper = [[None] * SUB for _ in range(SUB)]
    for j in range(SUB):
        inverse[j] = lax.rsqrt(rest[j][j])
        for k in range(j + 1, SUB):
            upper[j][k] = rest[j][k] * inverse[j]
        for i in range(j + 1, SUB):
            for k in range(i, SUB):
                rest[i][k] = rest[i][k] - upper[j][i] * upper[j][k]
    result = [[None] * SUB for _ in range(SUB)]
    for j in range(SUB):
        result[j][j] = inverse[j]
        for i in range(j + 1, SUB):
            total = upper[j][i] * result[j][j]
            for k in range(j + 1, i):
                total = total + upper[k][i] * result[k][j]
            result[i][j] = -(inverse[i] * total)
    return result


def in_three(value):
    first = value.astype(bf16)
    rest = value - first.astype(f32)
    second = rest.astype(bf16)
    return first, second, (rest - second.astype(f32)).astype(bf16)


def exact(left, right, left_dim, right_dim):
    a, b, c = in_three(left)
    d, e, f = in_three(right)
    lefts = jnp.concatenate([a, a, b, b, a, c], axis=left_dim)
    rights = jnp.concatenate([d, e, d, e, f, d], axis=right_dim)
    return product(lefts, rights, left_dim, right_dim)


def factor_block(held):
    sub = lax.broadcasted_iota(jnp.int32, (SUB, BLOCK), 0)
    lane = lax.broadcasted_iota(jnp.int32, (SUB, BLOCK), 1)
    lane_row = lax.broadcasted_iota(jnp.int32, (1, BLOCK), 1)
    rows = held[0:SUB, :]
    for lo in range(0, BLOCK, SUB):
        hi = lo + SUB
        lanes = [spread(rows[:, lo + k : lo + k + 1]) for k in range(SUB)]
        entries = [[spread(lanes[k][i : i + 1, :]) if k >= i else None for k in range(SUB)] for i in range(SUB)]
        inverse = small_inverse(entries)
        columns = []
        for k in range(SUB):
            column = jnp.zeros((SUB, BLOCK), f32)
            for i in range(k, SUB):
                column = jnp.where(sub == i, inverse[i][k], column)
            columns.append(column)
        inside = (lane >= lo) & (lane < hi)
        rows = jnp.where(inside, jnp.where(lane - lo == sub, 1.0, 0.0), rows)
        done = added([columns[k] * spread(rows[k : k + 1, :]) for k in range(SUB)])
        held[lo:hi, :] = done
        if hi < BLOCK:
            following = held[hi : hi + SUB, :]
            across = [spread(following[:, lo + k : lo + k + 1]) for k in range(SUB)]
            weights = [added([across[k] * inverse[i][k] for k in range(i + 1)]) for i in range(SUB)]
            rows = jnp.where(inside, 0.0, following) - added(
                [weights[i] * spread(done[i : i + 1, :]) for i in range(SUB)]
            )
        if hi + SUB < BLOCK:
            change = exact(done, done, 0, 0)
            kept = jnp.where((lane_row >= lo) & (lane_row < hi), 0.0, held[hi + SUB :, :])
            held[hi + SUB :, :] = kept - change[hi + SUB :, :]


def inverse_kernel(place_ref, own_ref, other_ref, high_ref, low_ref, gram, inverse, held):
    first = {pair: n * BLOCK for n, pair in enumerate(PAIRS)}
    for n in range(2 * FAR):
        source = own_ref if n < FAR else other_ref
        into = pl.multiple_of(place_ref[n] * SHARE, SUB)
        gram[pl.ds(into, SHARE), :] = source[(n % FAR) * SHARE : (n % FAR + 1) * SHARE, :]

    def block(i, j):
        return gram[first[i, j] : first[i, j] + BLOCK, :]

    inverse[...] = jnp.zeros((R, R), f32)
    row = lax.broadcasted_iota(jnp.int32, (BLOCK, BLOCK), 0)
    column = lax.broadcasted_iota(jnp.int32, (BLOCK, BLOCK), 1)
    for b in range(BLOCKS):
        lo, hi = b * BLOCK, (b + 1) * BLOCK
        held[...] = block(b, b)
        factor_block(held)
        own = jnp.where(column <= row, held[...], 0.0)
        if b:
            inverse[lo:hi, :lo] = exact(own, inverse[lo:hi, :lo], 1, 0)
        inverse[lo:hi, lo:hi] = own
        lower = {i: exact(block(i, b), own, 1, 1) for i in range(b + 1, BLOCKS)}
        for i in range(b + 1, BLOCKS):
            for j in range(b + 1, i + 1):
                gram[first[i, j] : first[i, j] + BLOCK, :] = block(i, j) - exact(lower[i], lower[j], 1, 1)
            into = slice(i * BLOCK, (i + 1) * BLOCK)
            inverse[into, :hi] = inverse[into, :hi] - exact(lower[i], inverse[lo:hi, :hi], 1, 0)
    high = inverse[...].astype(bf16)
    high_ref[...] = high
    low_ref[...] = (inverse[...] - high.astype(f32)).astype(bf16)


def inverse_factor(place, own, other):
    whole = pl.BlockSpec(memory_space=pltpu.VMEM)
    return pl.pallas_call(
        inverse_kernel,
        out_shape=[jax.ShapeDtypeStruct((R, R), bf16)] * 2,
        in_specs=[pl.BlockSpec(memory_space=pltpu.SMEM), whole, whole],
        out_specs=[whole] * 2,
        scratch_shapes=[
            pltpu.VMEM((len(PAIRS) * BLOCK, BLOCK), f32),
            pltpu.VMEM((R, R), f32),
            pltpu.VMEM((BLOCK, BLOCK), f32),
        ],
        compiler_params=pltpu.CompilerParams(vmem_limit_bytes=32 << 20),
        cost_estimate=pl.CostEstimate(flops=2 * R**3, bytes_accessed=2 << 20, transcendentals=R),
    )(place, own, other)


def from_everyone(value, axis):
    length = lax.axis_size(axis)
    return lax.all_to_all(jnp.broadcast_to(value[None], (length, *value.shape)), axis, 0, 0, tiled=True)


def from_ahead(value, axis, steps):
    length = lax.axis_size(axis)
    return lax.ppermute(value, axis, [(i, (i - steps) % length) for i in range(length)])


def ahead(value, axis):
    return [value] + [from_ahead(value, axis, steps) for steps in range(1, lax.axis_size(axis))]


def in_order(own, other, core):
    first = jnp.where(core == 0, own, other)
    second = jnp.where(core == 0, other, own)
    return jnp.concatenate([first, second])


def on_device(momentum, gradient, factor):
    z_hi, y, x, z_lo, core = (lax.axis_index(name) for name in ("z_hi", "y", "x", "z_lo", "core"))
    columns = factor.shape[1]
    lowered = factor.T.astype(bf16)
    across = from_ahead(lowered, "z_hi", 1)
    both = jnp.stack([jnp.where(z_hi == 0, lowered, across), jnp.where(z_hi == 0, across, lowered)])
    all_lowered = jnp.moveaxis(from_everyone(both, "y"), 0, 1).reshape(R, -1)
    blended = (momentum.astype(f32) + gradient.astype(f32)).astype(bf16)
    half = blended.shape[0] // 2
    own_rows = lax.dynamic_slice_in_dim(blended, core * half, half, 0)
    other_rows = lax.dynamic_slice_in_dim(blended, (1 - core) * half, half, 0)

    sent = product(other_rows, all_lowered, 1, 1).astype(bf16)
    arrived = from_ahead(sent, "core", 1)
    partial_left = (product(own_rows, all_lowered, 1, 1) + arrived.astype(f32)).astype(bf16)
    pieces = lax.all_to_all(partial_left.reshape(FAR, -1, R), ("x", "z_lo"), 0, 0, tiled=True)
    left_rows = jnp.sum(pieces.astype(f32), axis=0).astype(bf16)
    own_left = from_everyone(left_rows, ("x", "z_lo")).reshape(half, R)
    other_left = from_ahead(own_left, "core", 1)
    left_factor = in_order(own_left, other_left, core)

    partial_right = product(left_factor, blended, 0, 0).astype(bf16)
    received = lax.all_to_all(partial_right.reshape(8, columns, -1), ("z_hi", "y"), 0, 0, tiled=True)

    gram_left, _ = lax.optimization_barrier((left_factor, partial_right))
    local_gram = product(gram_left, gram_left, 0, 0)
    packed = jnp.concatenate(
        [local_gram[i * BLOCK : (i + 1) * BLOCK, j * BLOCK : (j + 1) * BLOCK] for i, j in PAIRS]
    )
    piece = lax.dynamic_slice_in_dim(packed, (core * FAR + z_lo * 4 + x) * SHARE, SHARE, 0)
    along = ahead(piece, "y")
    summed = sum(along[1:], along[0])
    summed = summed + from_ahead(summed, "z_hi", 1)
    line = jnp.concatenate(ahead(summed, "x"))
    received, line = lax.optimization_barrier((received, line))
    right_rows = jnp.sum(received.astype(f32), axis=0).astype(bf16)
    raw_right = from_everyone(right_rows, ("z_hi", "y")).reshape(R, -1)
    line, _ = lax.optimization_barrier((line, right_rows))
    own_gram = jnp.concatenate(ahead(line, "z_lo"))
    other_gram = from_ahead(own_gram, "core", 1)
    place = jnp.stack(
        [
            (core + c) % 2 * FAR + (z_lo + i) % 4 * 4 + (x + j) % 4
            for c in range(2)
            for i in range(4)
            for j in range(4)
        ]
    ).astype(jnp.int32)
    high, low = inverse_factor(place, own_gram, other_gram)

    right_factor = product(high, raw_right, 1, 0) + product(low, raw_right, 1, 0)
    square_sums = jnp.sum(from_everyone(jnp.sum(right_factor * right_factor, axis=1)[None], TENSOR), axis=(0, 1))
    orthonormal = (product(left_factor, high, 1, 1) + product(left_factor, low, 1, 1)).astype(bf16)
    inverse = lax.rsqrt(square_sums + epsilon)[:, None]
    full_factor = right_factor * inverse
    own_factor = lax.dynamic_slice_in_dim(full_factor, (z_hi * 4 + y) * columns, columns, 0).T
    taken = product(orthonormal, right_factor.astype(bf16), 1, 0)
    stepped = product(orthonormal, full_factor.astype(bf16), 1, 0)
    new_momentum = (blended.astype(f32) - (1.0 - decay_rate) * taken).astype(bf16)
    update = (stepped * jnp.sqrt(f32(D * FF / R))).astype(bf16)
    return (new_momentum, own_factor, update)


def solution(mesh):
    torus = Mesh(mesh.devices.reshape(2, 4, 4, 4, 2), ("z_hi", "y", "x", "z_lo", "core"))
    fsdp = ("z_hi", "y")
    return jax.shard_map(
        on_device,
        mesh=torus,
        in_specs=(P(fsdp, TENSOR), P(fsdp, TENSOR), P(TENSOR, fsdp)),
        out_specs=(P(fsdp, TENSOR), P(TENSOR, fsdp), P(fsdp, TENSOR)),
        check_vma=False,
    )
```

profile of v0, /device:TPU:1, one launch (start us, length us, event | category | flops | bytes accessed | tf_op | source)
XLA Modules:
  0.0 208.4 jit_solution(9264101505805037710)
XLA Ops:
  0.6 1.0 convert_bitcast_fusion
  1.6 7.8 %collective-permute-start = (bf16[64,896]{1,0:T(8,128)(2,1)S(1)}, bf16[64,896]{1,0:T(8,128)(2,1)S(1)}, u32[]{:S(2)}, u32[]{:S(2)}) collective-permute-start(bf16[64,896]{1,0:T(8,128)(2,1)S(1)} %convert_bitcast_fusion), channel_id=1, source_target_pairs={{0,128},{128,0},{1,129},{129,1},{2,130},{130,2},{3,131},{131,3},{4... | collective-permute-start | bytes 344072 | tf_op jit(solution)/shard_map/ppermute | solution.py:168
  9.4 2.3 %collective-permute-done = bf16[64,896]{1,0:T(8,128)(2,1)S(1)} collective-permute-done((bf16[64,896]{1,0:T(8,128)(2,1)S(1)}, bf16[64,896]{1,0:T(8,128)(2,1)S(1)}, u32[]{:S(2)}, u32[]{:S(2)}) %collective-permute-start) | collective-permute-done | bytes 114720 | tf_op jit(solution)/shard_map/ppermute | solution.py:168
  11.7 1.0 select_bitcast_fusion.1
  12.7 1.0 broadcast_in_dim.8
  13.8 4.8 %all-to-all-start = ((bf16[4,2,64,896]{3,2,1,0:T(8,128)(2,1)}), bf16[4,2,64,896]{3,2,1,0:T(8,128)(2,1)S(1)}, u32[]{:S(2)}, u32[]{:S(2)}) async-start(bf16[4,2,64,896]{3,2,1,0:T(8,128)(2,1)} %broadcast_in_dim.8), calls=%async_computation | async-start | bytes 1835008 | tf_op jit(solution)/shard_map/all_to_all | solution.py:163
  18.5 3.2 %add_convert_fusion = bf16[1024,896]{1,0:T(8,128)(2,1)} fusion(bf16[1024,896]{1,0:T(8,128)(2,1)S(1)} %copy-done, bf16[1024,896]{1,0:T(8,128)(2,1)} %param.3), kind=kLoop, calls=%fused_computation.2 | loop fusion | flops 3670016 | bytes 5505024 | tf_op jit(solution)/shard_map/convert_element_type | solution.py:188
  21.7 8.9 %all-to-all-done = bf16[4,2,64,896]{3,2,1,0:T(8,128)(2,1)S(1)} async-done(((bf16[4,2,64,896]{3,2,1,0:T(8,128)(2,1)}), bf16[4,2,64,896]{3,2,1,0:T(8,128)(2,1)S(1)}, u32[]{:S(2)}, u32[]{:S(2)}) %all-to-all-start) | async-done | bytes 917536 | tf_op jit(solution)/shard_map/all_to_all | solution.py:163
  30.7 0.9 copy-done.3
  31.7 0.7 convolution_convert_fusion.1
  32.4 2.6 %collective-permute-start.1 = (bf16[512,512]{1,0:T(8,128)(2,1)S(1)}, bf16[512,512]{1,0:T(8,128)(2,1)S(1)}, u32[]{:S(2)}, u32[]{:S(2)}) collective-permute-start(bf16[512,512]{1,0:T(8,128)(2,1)S(1)} %convolution_convert_fusion.1), channel_id=1, source_target_pairs={{0,1},{1,0},{2,3},{3,2},{4,5},{5,4},{6,7},{7,6},{8,9},{9,8},{10,11... | collective-permute-start | bytes 1572872 | tf_op jit(solution)/shard_map/ppermute | solution.py:168
  35.0 1.5 collective-permute-done.1
  36.6 1.9 add_convert_fusion.2
  38.5 23.4 %all_to_all.30 = bf16[16,32,512]{2,1,0:T(8,128)(2,1)S(1)} all-to-all(bf16[16,32,512]{2,1,0:T(8,128)(2,1)S(1)} %bitcast.68), channel_id=1, replica_groups=mesh['z_hi'=2,'y'=4,'x'=4,'z_lo'=4,'core'=2] {'x','z_lo'}, dimensions={0} | all-to-all | bytes 1048576 | tf_op jit(solution)/shard_map/all_to_all | solution.py:196
  62.0 19.6 %all_to_all.31 = bf16[16,32,512]{2,1,0:T(8,128)(2,1)S(1)} all-to-all(bf16[16,32,512]{2,1,0:T(8,128)(2,1)S(1)} %broadcast_in_dim.9), channel_id=1, replica_groups=mesh['z_hi'=2,'y'=4,'x'=4,'z_lo'=4,'core'=2] {'x','z_lo'}, dimensions={0} | all-to-all | bytes 1048576 | tf_op jit(solution)/shard_map/all_to_all | solution.py:163
  81.6 1.7 collective-permute-start.2
  83.4 1.5 collective-permute-done.2
  85.0 3.7 %convolution_convert_fusion = bf16[512,896]{1,0:T(8,128)(2,1)} fusion(bf16[1024,896]{1,0:T(8,128)(2,1)} %add_convert_fusion, bf16[512,512]{1,0:T(8,128)(2,1)S(1)} %get-tuple-element.16, bf16[512,512]{1,0:T(8,128)(2,1)S(1)} %get-tuple-element.15), kind=kOutput, calls=%fused_computation.6 | convolution fusion | flops 942080000 | bytes 3801088 | tf_op jit(solution)/shard_map/dot_general | solution.py:27
  88.7 1.0 pad_maximum_fusion
  89.8 6.7 %all-to-all-start.3 = ((bf16[8,64,896]{2,1,0:T(8,128)(2,1)}), bf16[8,64,896]{2,1,0:T(8,128)(2,1)S(1)}, u32[]{:S(2)}, u32[]{:S(2)}) async-start(bf16[8,64,896]{2,1,0:T(8,128)(2,1)} %bitcast.65), calls=%async_computation.3 | async-start | bytes 1835008 | tf_op jit(solution)/shard_map/all_to_all | solution.py:203
  96.5 2.4 %fusion.10 = f32[512,512]{1,0:T(8,128)S(1)} fusion(bf16[1024,512]{1,0:T(8,128)(2,1)} %pad_maximum_fusion), kind=kOutput, calls=%fused_computation.43 | convolution fusion | flops 536870912 | bytes 2097152 | tf_op jit(solution)/shard_map/dot_general | solution.py:27
  99.0 1.5 collective-permute-start.5
  100.6 2.4 %collective-permute-start.4 = (f32[40,128]{1,0:T(8,128)S(1)}, f32[40,128]{1,0:T(8,128)S(1)}, u32[]{:S(2)}, u32[]{:S(2)}) collective-permute-start(f32[40,128]{1,0:T(8,128)S(1)} %constant_dynamic-slice_fusion), channel_id=1, source_target_pairs={{0,64},{32,96},{64,0},{96,32},{1,65},{33,97},{65,1},{97,33},{2,66}... | collective-permute-start | bytes 61448 | tf_op jit(solution)/shard_map/ppermute | solution.py:168
  103.0 1.2 collective-permute-start.3
  104.1 1.6 collective-permute-done.5
  105.7 1.4 collective-permute-done.3
  107.1 7.1 %collective-permute-start.6 = (f32[40,128]{1,0:T(8,128)S(1)}, f32[40,128]{1,0:T(8,128)S(1)}, u32[]{:S(2)}, u32[]{:S(2)}) collective-permute-start(f32[40,128]{1,0:T(8,128)S(1)} %add_add_fusion), channel_id=1, source_target_pairs={{0,128},{128,0},{1,129},{129,1},{2,130},{130,2},{3,131},{131,3},{4... | collective-permute-start | bytes 61448 | tf_op jit(solution)/shard_map/ppermute | solution.py:168
  114.3 5.5 %collective-permute-done.6 = f32[40,128]{1,0:T(8,128)S(1)} collective-permute-done((f32[40,128]{1,0:T(8,128)S(1)}, f32[40,128]{1,0:T(8,128)S(1)}, u32[]{:S(2)}, u32[]{:S(2)}) %collective-permute-start.6) | collective-permute-done | bytes 20512 | tf_op jit(solution)/shard_map/ppermute | solution.py:168
  119.8 1.9 collective-permute-start.9
  122.1 2.1 collective-permute-start.7
  124.1 1.7 collective-permute-done.8
  126.0 1.1 broadcast_in_dim.10
  127.1 8.5 %all-to-all-start.4 = ((bf16[8,64,896]{2,1,0:T(8,128)(2,1)}), bf16[8,64,896]{2,1,0:T(8,128)(2,1)}, u32[]{:S(2)}, u32[]{:S(2)}) async-start(bf16[8,64,896]{2,1,0:T(8,128)(2,1)} %broadcast_in_dim.10), calls=%async_computation.4 | async-start | bytes 1835008 | tf_op jit(solution)/shard_map/all_to_all | solution.py:163
  135.6 2.7 %collective-permute-start.10 = (f32[160,128]{1,0:T(8,128)S(1)}, f32[160,128]{1,0:T(8,128)S(1)}, u32[]{:S(2)}, u32[]{:S(2)}) collective-permute-start(f32[160,128]{1,0:T(8,128)S(1)} %pad_maximum_fusion.2), channel_id=1, source_target_pairs={{0,6},{2,0},{4,2},{6,4},{1,7},{3,1},{5,3},{7,5},{8,14},{10,8},{12,... | collective-permute-start | bytes 245768 | tf_op jit(solution)/shard_map/ppermute | solution.py:168
  138.8 17.4 %collective-permute-done.10 = f32[160,128]{1,0:T(8,128)S(1)} collective-permute-done((f32[160,128]{1,0:T(8,128)S(1)}, f32[160,128]{1,0:T(8,128)S(1)}, u32[]{:S(2)}, u32[]{:S(2)}) %collective-permute-start.10) | collective-permute-done | bytes 81952 | tf_op jit(solution)/shard_map/ppermute | solution.py:168
  156.2 7.8 %collective-permute-done.11 = f32[160,128]{1,0:T(8,128)S(1)} collective-permute-done((f32[160,128]{1,0:T(8,128)S(1)}, f32[160,128]{1,0:T(8,128)S(1)}, u32[]{:S(2)}, u32[]{:S(2)}) %collective-permute-start.11) | collective-permute-done | bytes 81952 | tf_op jit(solution)/shard_map/ppermute | solution.py:168
  164.7 1.1 collective-permute-done.13.other_ref
  165.8 18.3 %shard_map.58 = (bf16[512,512]{1,0:T(8,128)(2,1)S(1)}, bf16[512,512]{1,0:T(8,128)(2,1)S(1)}) custom-call(s32[32]{0:T(128)S(1)} %stack.143.place_ref, f32[640,128]{1,0:T(8,128)S(1)} %constant_dynamic-update-slice_fusion.own_ref, f32[640,128]{1,0:T(8,128)S(1)} %collective-permute-done.13.other_ref), custom_call_target="tpu_custom_call" | custom-call | flops 268435456 | bytes 2097152 | tf_op jit(solution)/shard_map/pallas_call | solution.py:146
  184.2 0.9 fusion.9
  185.1 1.7 add_convert_fusion.1
  186.8 1.9 fusion.11
  188.7 2.1 multiply_reduce_fusion
  190.8 0.7 broadcast_in_dim.11
  191.5 5.7 %all-to-all-start.5 = ((f32[32,1,512]{2,1,0:T(1,128)}), f32[32,1,512]{2,1,0:T(1,128)S(1)}, u32[]{:S(2)}, u32[]{:S(2)}) async-start(f32[32,1,512]{2,1,0:T(1,128)} %broadcast_in_dim.11), calls=%async_computation.5 | async-start | bytes 131072 | tf_op jit(solution)/shard_map/all_to_all | solution.py:163
  197.2 4.0 %subtract_convert_fusion = bf16[1024,896]{1,0:T(8,128)(2,1)} fusion(bf16[1024,896]{1,0:T(8,128)(2,1)} %add_convert_fusion, bf16[1024,512]{1,0:T(8,128)(2,1)S(1)} %copy-done.2, f32[512,896]{1,0:T(8,128)S(1)} %get-tuple-element.20), kind=kOutput, calls=%fused_computation.1 | convolution fusion | flops 943652864 | bytes 6553600 | tf_op jit(solution)/shard_map/dot_general | solution.py:27
  201.2 3.8 %all-to-all-done.5 = f32[32,1,512]{2,1,0:T(1,128)S(1)} async-done(((f32[32,1,512]{2,1,0:T(1,128)}), f32[32,1,512]{2,1,0:T(1,128)S(1)}, u32[]{:S(2)}, u32[]{:S(2)}) %all-to-all-start.5) | async-done | bytes 65568 | tf_op jit(solution)/shard_map/all_to_all | solution.py:163
  205.3 2.5 %multiply_convert_fusion = bf16[1024,896]{1,0:T(8,128)(2,1)} fusion(bf16[1024,512]{1,0:T(8,128)(2,1)S(1)} %copy-done.2, f32[512,896]{1,0:T(8,128)S(1)} %broadcast_multiply_fusion), kind=kOutput, calls=%fused_computation | convolution fusion | flops 941817856 | bytes 4718592 | tf_op jit(solution)/shard_map/dot_general | solution.py:27
  207.7 0.7 dynamic-slice_bitcast_fusion
  (44 shorter events, 2.5 us)
Async XLA Ops:
  1.6 10.1 %collective-permute-start = (bf16[64,896]{1,0:T(8,128)(2,1)S(1)}, bf16[64,896]{1,0:T(8,128)(2,1)S(1)}, u32[]{:S(2)}, u32[]{:S(2)}) collective-permute-start(bf16[64,896]{1,0:T(8,128)(2,1)S(1)} %convert_bitcast_fusion), channel_id=1, source_target_pairs={{0,128},{128,0},{1,129},{129,1},{2,130},{130,2},{3,131},{131,3},{4... | collective-permute-start | bytes 344072 | tf_op jit(solution)/shard_map/ppermute | solution.py:168
  12.7 5.9 %copy-start = (bf16[1024,896]{1,0:T(8,128)(2,1)S(1)}, bf16[1024,896]{1,0:T(8,128)(2,1)}, u32[]{:S(2)}) copy-start(bf16[1024,896]{1,0:T(8,128)(2,1)} %param.4) | copy-start | bytes 5505028
  13.8 16.9 %all-to-all-start = ((bf16[4,2,64,896]{3,2,1,0:T(8,128)(2,1)}), bf16[4,2,64,896]{3,2,1,0:T(8,128)(2,1)S(1)}, u32[]{:S(2)}, u32[]{:S(2)}) async-start(bf16[4,2,64,896]{3,2,1,0:T(8,128)(2,1)} %broadcast_in_dim.8), calls=%async_computation | async-start | bytes 1835008 | tf_op jit(solution)/shard_map/all_to_all | solution.py:163
  21.7 9.9 %copy-start.1 = (bf16[1024,896]{1,0:T(8,128)(2,1)S(1)}, bf16[1024,896]{1,0:T(8,128)(2,1)}, u32[]{:S(2)}) copy-start(bf16[1024,896]{1,0:T(8,128)(2,1)} %add_convert_fusion) | copy-start | bytes 5505028
  30.7 0.9 copy-start.3
  32.4 4.2 %collective-permute-start.1 = (bf16[512,512]{1,0:T(8,128)(2,1)S(1)}, bf16[512,512]{1,0:T(8,128)(2,1)S(1)}, u32[]{:S(2)}, u32[]{:S(2)}) collective-permute-start(bf16[512,512]{1,0:T(8,128)(2,1)S(1)} %convolution_convert_fusion.1), channel_id=1, source_target_pairs={{0,1},{1,0},{2,3},{3,2},{4,5},{5,4},{6,7},{7,6},{8,9},{9,8},{10,11... | collective-permute-start | bytes 1572872 | tf_op jit(solution)/shard_map/ppermute | solution.py:168
  81.6 3.3 %collective-permute-start.2 = (bf16[512,512]{1,0:T(8,128)(2,1)S(1)}, bf16[512,512]{1,0:T(8,128)(2,1)S(1)}, u32[]{:S(2)}, u32[]{:S(2)}) collective-permute-start(bf16[512,512]{1,0:T(8,128)(2,1)S(1)} %bitcast.64), channel_id=1, source_target_pairs={{0,1},{1,0},{2,3},{3,2},{4,5},{5,4},{6,7},{7,6},{8,9},{9,8},{10,11... | collective-permute-start | bytes 1572872 | tf_op jit(solution)/shard_map/ppermute | solution.py:168
  89.8 36.0 %all-to-all-start.3 = ((bf16[8,64,896]{2,1,0:T(8,128)(2,1)}), bf16[8,64,896]{2,1,0:T(8,128)(2,1)S(1)}, u32[]{:S(2)}, u32[]{:S(2)}) async-start(bf16[8,64,896]{2,1,0:T(8,128)(2,1)} %bitcast.65), calls=%async_computation.3 | async-start | bytes 1835008 | tf_op jit(solution)/shard_map/all_to_all | solution.py:203
  99.0 6.7 %collective-permute-start.5 = (f32[40,128]{1,0:T(8,128)S(1)}, f32[40,128]{1,0:T(8,128)S(1)}, u32[]{:S(2)}, u32[]{:S(2)}) collective-permute-start(f32[40,128]{1,0:T(8,128)S(1)} %constant_dynamic-slice_fusion), channel_id=1, source_target_pairs={{0,32},{32,64},{64,96},{96,0},{1,33},{33,65},{65,97},{97,1},{2,34}... | collective-permute-start | bytes 61448 | tf_op jit(solution)/shard_map/ppermute | solution.py:168
  100.6 5.2 %collective-permute-start.4 = (f32[40,128]{1,0:T(8,128)S(1)}, f32[40,128]{1,0:T(8,128)S(1)}, u32[]{:S(2)}, u32[]{:S(2)}) collective-permute-start(f32[40,128]{1,0:T(8,128)S(1)} %constant_dynamic-slice_fusion), channel_id=1, source_target_pairs={{0,64},{32,96},{64,0},{96,32},{1,65},{33,97},{65,1},{97,33},{2,66}... | collective-permute-start | bytes 61448 | tf_op jit(solution)/shard_map/ppermute | solution.py:168
  103.0 4.2 %collective-permute-start.3 = (f32[40,128]{1,0:T(8,128)S(1)}, f32[40,128]{1,0:T(8,128)S(1)}, u32[]{:S(2)}, u32[]{:S(2)}) collective-permute-start(f32[40,128]{1,0:T(8,128)S(1)} %constant_dynamic-slice_fusion), channel_id=1, source_target_pairs={{0,96},{32,0},{64,32},{96,64},{1,97},{33,1},{65,33},{97,65},{2,98}... | collective-permute-start | bytes 61448 | tf_op jit(solution)/shard_map/ppermute | solution.py:168
  107.1 12.6 %collective-permute-start.6 = (f32[40,128]{1,0:T(8,128)S(1)}, f32[40,128]{1,0:T(8,128)S(1)}, u32[]{:S(2)}, u32[]{:S(2)}) collective-permute-start(f32[40,128]{1,0:T(8,128)S(1)} %add_add_fusion), channel_id=1, source_target_pairs={{0,128},{128,0},{1,129},{129,1},{2,130},{130,2},{3,131},{131,3},{4... | collective-permute-start | bytes 61448 | tf_op jit(solution)/shard_map/ppermute | solution.py:168
  119.8 4.3 %collective-permute-start.9 = (f32[40,128]{1,0:T(8,128)S(1)}, f32[40,128]{1,0:T(8,128)S(1)}, u32[]{:S(2)}, u32[]{:S(2)}) collective-permute-start(f32[40,128]{1,0:T(8,128)S(1)} %add.461), channel_id=1, source_target_pairs={{0,8},{8,16},{16,24},{24,0},{1,9},{9,17},{17,25},{25,1},{2,10},{10... | collective-permute-start | bytes 61448 | tf_op jit(solution)/shard_map/ppermute | solution.py:168
  121.6 4.1 %collective-permute-start.8 = (f32[40,128]{1,0:T(8,128)S(1)}, f32[40,128]{1,0:T(8,128)S(1)}, u32[]{:S(2)}, u32[]{:S(2)}) collective-permute-start(f32[40,128]{1,0:T(8,128)S(1)} %add.461), channel_id=1, source_target_pairs={{0,16},{8,24},{16,0},{24,8},{1,17},{9,25},{17,1},{25,9},{2,18},{10... | collective-permute-start | bytes 61448 | tf_op jit(solution)/shard_map/ppermute | solution.py:168
  122.1 3.7 %collective-permute-start.7 = (f32[40,128]{1,0:T(8,128)S(1)}, f32[40,128]{1,0:T(8,128)S(1)}, u32[]{:S(2)}, u32[]{:S(2)}) collective-permute-start(f32[40,128]{1,0:T(8,128)S(1)} %add.461), channel_id=1, source_target_pairs={{0,24},{8,0},{16,8},{24,16},{1,25},{9,1},{17,9},{25,17},{2,26},{10... | collective-permute-start | bytes 61448 | tf_op jit(solution)/shard_map/ppermute | solution.py:168
  127.1 59.8 %all-to-all-start.4 = ((bf16[8,64,896]{2,1,0:T(8,128)(2,1)}), bf16[8,64,896]{2,1,0:T(8,128)(2,1)}, u32[]{:S(2)}, u32[]{:S(2)}) async-start(bf16[8,64,896]{2,1,0:T(8,128)(2,1)} %broadcast_in_dim.10), calls=%async_computation.4 | async-start | bytes 1835008 | tf_op jit(solution)/shard_map/all_to_all | solution.py:163
  135.6 20.7 %collective-permute-start.10 = (f32[160,128]{1,0:T(8,128)S(1)}, f32[160,128]{1,0:T(8,128)S(1)}, u32[]{:S(2)}, u32[]{:S(2)}) collective-permute-start(f32[160,128]{1,0:T(8,128)S(1)} %pad_maximum_fusion.2), channel_id=1, source_target_pairs={{0,6},{2,0},{4,2},{6,4},{1,7},{3,1},{5,3},{7,5},{8,14},{10,8},{12,... | collective-permute-start | bytes 245768 | tf_op jit(solution)/shard_map/ppermute | solution.py:168
  138.3 25.8 %collective-permute-start.11 = (f32[160,128]{1,0:T(8,128)S(1)}, f32[160,128]{1,0:T(8,128)S(1)}, u32[]{:S(2)}, u32[]{:S(2)}) collective-permute-start(f32[160,128]{1,0:T(8,128)S(1)} %pad_maximum_fusion.2), channel_id=1, source_target_pairs={{0,4},{2,6},{4,0},{6,2},{1,5},{3,7},{5,1},{7,3},{8,12},{10,14},{12... | collective-permute-start | bytes 245768 | tf_op jit(solution)/shard_map/ppermute | solution.py:168
  138.3 25.8 %collective-permute-start.12 = (f32[160,128]{1,0:T(8,128)S(1)}, f32[160,128]{1,0:T(8,128)S(1)}, u32[]{:S(2)}, u32[]{:S(2)}) collective-permute-start(f32[160,128]{1,0:T(8,128)S(1)} %pad_maximum_fusion.2), channel_id=1, source_target_pairs={{0,2},{2,4},{4,6},{6,0},{1,3},{3,5},{5,7},{7,1},{8,10},{10,12},{12... | collective-permute-start | bytes 245768 | tf_op jit(solution)/shard_map/ppermute | solution.py:168
  164.1 1.8 collective-permute-start.13
  188.7 8.5 %copy-start.2 = (bf16[1024,512]{1,0:T(8,128)(2,1)S(1)}, bf16[1024,512]{1,0:T(8,128)(2,1)}, u32[]{:S(2)}) copy-start(bf16[1024,512]{1,0:T(8,128)(2,1)} %add_convert_fusion.1) | copy-start | bytes 3145732
  191.5 13.5 %all-to-all-start.5 = ((f32[32,1,512]{2,1,0:T(1,128)}), f32[32,1,512]{2,1,0:T(1,128)S(1)}, u32[]{:S(2)}, u32[]{:S(2)}) async-start(f32[32,1,512]{2,1,0:T(1,128)} %broadcast_in_dim.11), calls=%async_computation.5 | async-start | bytes 131072 | tf_op jit(solution)/shard_map/all_to_all | solution.py:163
where the time goes:
time: 209 us; the launch traced here: 208 us
  starting transfers between devices  58.1 us (28%)
  waiting for transfers between devices  54.6 us (26%)
  blocking collectives  43 us (21%)
  matrix products  21.8 us (10%)
  Pallas kernels  18.3 us (9%)
  other arithmetic  6.76 us (3%)
  local copies, waits for them, and re-layouts  4.83 us (2%)
    ppermute x14, waiting for transfers between devices, from_ahead(): lax.ppermute(value, axis, [(i, (i - steps) % length) for i in range(lengt...  41.9 us
    ppermute x14, starting transfers between devices, from_ahead(): lax.ppermute(value, axis, [(i, (i - steps) % length) for i in range(lengt...  32.5 us
    all_to_all x1, blocking collectives, on_device(): lax.all_to_all(partial_left.reshape(FAR, -1, R), ('x', 'z_lo'), 0, 0, til...  23.4 us
    dot_general x10, matrix products, product(): lax.dot_general(left, right, (((left_dim,), (right_dim,)), ((), ())), pre...  21.8 us
    all_to_all x1, blocking collectives, from_everyone(): lax.all_to_all(jnp.broadcast_to(value[None], (length, *value.shape)), axi...  19.6 us
    all_to_all x3, starting transfers between devices, from_everyone(): lax.all_to_all(jnp.broadcast_to(value[None], (length, *value.shape)), axi...  19 us
    pallas_call x1, Pallas kernels, inverse_factor(): pl.pallas_call(inverse_kernel, out_shape=[jax.ShapeDtypeStruct((R, R), bf...  18.3 us
    all_to_all x3, waiting for transfers between devices, from_everyone(): lax.all_to_all(jnp.broadcast_to(value[None], (length, *value.shape)), axi...  12.7 us
  transfers between devices with their start and end apart: 18, of which 12 were waited for; matrix products, arithmetic and copies ran while one was open for 6% of the time, Pallas kernels for 9%

commit v1 on v0

--- a/solution.py
+++ b/solution.py
@@ -15,6 +15,8 @@
 PAIRS = [(i, j) for i in range(BLOCKS) for j in range(i + 1)]
 SHARE = len(PAIRS) * BLOCK // (2 * FAR)
 SUB = 8
+HALF = BLOCKS // 2
+LATER = [(i, j) for i, j in PAIRS if j >= HALF]
 TENSOR = ("x", "z_lo", "core")
 
 decay_rate = 0.95
@@ -109,53 +111,67 @@
             held[hi + SUB :, :] = kept - change[hi + SUB :, :]
 
 
-def inverse_kernel(place_ref, own_ref, other_ref, high_ref, low_ref, gram, inverse, held):
-    first = {pair: n * BLOCK for n, pair in enumerate(PAIRS)}
+FIRST = {pair: n * BLOCK for n, pair in enumerate(PAIRS)}
+
+
+def eliminate(b, stored, gram, inverse, held):
+    row = lax.broadcasted_iota(jnp.int32, (BLOCK, BLOCK), 0)
+    column = lax.broadcasted_iota(jnp.int32, (BLOCK, BLOCK), 1)
+
+    def block(i, j):
+        return gram[stored[i, j] : stored[i, j] + BLOCK, :]
+
+    lo, hi = b * BLOCK, (b + 1) * BLOCK
+    held[...] = block(b, b)
+    factor_block(held)
+    own = jnp.where(column <= row, held[...], 0.0)
+    if b:
+        inverse[lo:hi, :lo] = exact(own, inverse[lo:hi, :lo], 1, 0)
+    inverse[lo:hi, lo:hi] = own
+    lower = {i: exact(block(i, b), own, 1, 1) for i in range(b + 1, BLOCKS)}
+    for i in range(b + 1, BLOCKS):
+        for j in range(b + 1, i + 1):
+            gram[stored[i, j] : stored[i, j] + BLOCK, :] = block(i, j) - exact(lower[i], lower[j], 1, 1)
+        into = slice(i * BLOCK, (i + 1) * BLOCK)
+        inverse[into, :hi] = inverse[into, :hi] - exact(lower[i], inverse[lo:hi, :hi], 1, 0)
+
+
+def first_kernel(place_ref, own_ref, other_ref, rest_ref, inverse, gram, held):
     for n in range(2 * FAR):
         source = own_ref if n < FAR else other_ref
         into = pl.multiple_of(place_ref[n] * SHARE, SUB)
         gram[pl.ds(into, SHARE), :] = source[(n % FAR) * SHARE : (n % FAR + 1) * SHARE, :]
-
-    def block(i, j):
-        return gram[first[i, j] : first[i, j] + BLOCK, :]
-
-    inverse[...] = jnp.zeros((R, R), f32)
-    row = lax.broadcasted_iota(jnp.int32, (BLOCK, BLOCK), 0)
-    column = lax.broadcasted_iota(jnp.int32, (BLOCK, BLOCK), 1)
-    for b in range(BLOCKS):
-        lo, hi = b * BLOCK, (b + 1) * BLOCK
-        held[...] = block(b, b)
-        factor_block(held)
-        own = jnp.where(column <= row, held[...], 0.0)
-        if b:
-            inverse[lo:hi, :lo] = exact(own, inverse[lo:hi, :lo], 1, 0)
-        inverse[lo:hi, lo:hi] = own
-        lower = {i: exact(block(i, b), own, 1, 1) for i in range(b + 1, BLOCKS)}
-        for i in range(b + 1, BLOCKS):
-            for j in range(b + 1, i + 1):
-                gram[first[i, j] : first[i, j] + BLOCK, :] = block(i, j) - exact(lower[i], lower[j], 1, 1)
-            into = slice(i * BLOCK, (i + 1) * BLOCK)
-            inverse[into, :hi] = inverse[into, :hi] - exact(lower[i], inverse[lo:hi, :hi], 1, 0)
+    inverse[...] = jnp.zeros_like(inverse)
+    for b in range(HALF):
+        eliminate(b, FIRST, gram, inverse, held)
+    for n, pair in enumerate(LATER):
+        rest_ref[n * BLOCK : (n + 1) * BLOCK, :] = gram[FIRST[pair] : FIRST[pair] + BLOCK, :]
+
+
+def second_kernel(rest_ref, begun_ref, high_ref, low_ref, inverse, gram, held):
+    gram[...] = rest_ref[...]
+    inverse[:, : HALF * BLOCK] = begun_ref[...]
+    inverse[:, HALF * BLOCK :] = jnp.zeros((R, R - HALF * BLOCK), f32)
+    stored = {pair: n * BLOCK for n, pair in enumerate(LATER)}
+    for b in range(HALF, BLOCKS):
+        eliminate(b, stored, gram, inverse, held)
     high = inverse[...].astype(bf16)
     high_ref[...] = high
     low_ref[...] = (inverse[...] - high.astype(f32)).astype(bf16)
 
 
-def inverse_factor(place, own, other):
+def block_call(kernel, inputs, outputs, scratch):
     whole = pl.BlockSpec(memory_space=pltpu.VMEM)
+    small = pl.BlockSpec(memory_space=pltpu.SMEM)
     return pl.pallas_call(
-        inverse_kernel,
-        out_shape=[jax.ShapeDtypeStruct((R, R), bf16)] * 2,
-        in_specs=[pl.BlockSpec(memory_space=pltpu.SMEM), whole, whole],
-        out_specs=[whole] * 2,
-        scratch_shapes=[
-            pltpu.VMEM((len(PAIRS) * BLOCK, BLOCK), f32),
-            pltpu.VMEM((R, R), f32),
-            pltpu.VMEM((BLOCK, BLOCK), f32),
-        ],
+        kernel,
+        out_shape=[jax.ShapeDtypeStruct(shape, dtype) for shape, dtype in outputs],
+        in_specs=[whole if value.dtype == f32 else small for value in inputs],
+        out_specs=[whole] * len(outputs),
+        scratch_shapes=[pltpu.VMEM(shape, f32) for shape in scratch],
         compiler_params=pltpu.CompilerParams(vmem_limit_bytes=32 << 20),
-        cost_estimate=pl.CostEstimate(flops=2 * R**3, bytes_accessed=2 << 20, transcendentals=R),
-    )(place, own, other)
+        cost_estimate=pl.CostEstimate(flops=10 * R**3, bytes_accessed=2 << 20, transcendentals=R),
+    )(*inputs)
 
 
 def from_everyone(value, axis):
@@ -199,23 +215,18 @@
     other_left = from_ahead(own_left, "core", 1)
     left_factor = in_order(own_left, other_left, core)
 
-    partial_right = product(left_factor, blended, 0, 0).astype(bf16)
-    received = lax.all_to_all(partial_right.reshape(8, columns, -1), ("z_hi", "y"), 0, 0, tiled=True)
-
-    gram_left, _ = lax.optimization_barrier((left_factor, partial_right))
-    local_gram = product(gram_left, gram_left, 0, 0)
+    local_gram = product(left_factor, left_factor, 0, 0)
     packed = jnp.concatenate(
         [local_gram[i * BLOCK : (i + 1) * BLOCK, j * BLOCK : (j + 1) * BLOCK] for i, j in PAIRS]
     )
     piece = lax.dynamic_slice_in_dim(packed, (core * FAR + z_lo * 4 + x) * SHARE, SHARE, 0)
-    along = ahead(piece, "y")
-    summed = sum(along[1:], along[0])
-    summed = summed + from_ahead(summed, "z_hi", 1)
+    summed = jnp.sum(from_everyone(piece, ("z_hi", "y")), axis=0)
+
+    partial_right = product(left_factor, blended, 0, 0).astype(bf16)
+    summed, partial_right = lax.optimization_barrier((summed, partial_right))
+    received = lax.all_to_all(partial_right.reshape(4, R // 4, -1), "y", 0, 0, tiled=True)
+
     line = jnp.concatenate(ahead(summed, "x"))
-    received, line = lax.optimization_barrier((received, line))
-    right_rows = jnp.sum(received.astype(f32), axis=0).astype(bf16)
-    raw_right = from_everyone(right_rows, ("z_hi", "y")).reshape(R, -1)
-    line, _ = lax.optimization_barrier((line, right_rows))
     own_gram = jnp.concatenate(ahead(line, "z_lo"))
     other_gram = from_ahead(own_gram, "core", 1)
     place = jnp.stack(
@@ -226,11 +237,33 @@
             for j in range(4)
         ]
     ).astype(jnp.int32)
-    high, low = inverse_factor(place, own_gram, other_gram)
+
+    received, other_gram = lax.optimization_barrier((received, other_gram))
+    right_rows = jnp.sum(received.astype(f32), axis=0).astype(bf16)
+    other_gram, right_rows = lax.optimization_barrier((other_gram, right_rows))
+    opposite = from_ahead(right_rows, "z_hi", 1)
+    rest, begun = block_call(
+        first_kernel,
+        (place, own_gram, other_gram),
+        [((len(LATER) * BLOCK, BLOCK), f32), ((R, HALF * BLOCK), f32)],
+        [(len(PAIRS) * BLOCK, BLOCK), (BLOCK, BLOCK)],
+    )
+    opposite, rest = lax.optimization_barrier((opposite, rest))
+    right_rows = (right_rows.astype(f32) + opposite.astype(f32)).astype(bf16)
+    rest, right_rows = lax.optimization_barrier((rest, right_rows))
+    raw_right = from_everyone(right_rows, "y").reshape(R, -1)
+    high, low = block_call(
+        second_kernel,
+        (rest, begun),
+        [((R, R), bf16)] * 2,
+        [(R, R), (len(LATER) * BLOCK, BLOCK), (BLOCK, BLOCK)],
+    )
 
     right_factor = product(high, raw_right, 1, 0) + product(low, raw_right, 1, 0)
-    square_sums = jnp.sum(from_everyone(jnp.sum(right_factor * right_factor, axis=1)[None], TENSOR), axis=(0, 1))
-    orthonormal = (product(left_factor, high, 1, 1) + product(left_factor, low, 1, 1)).astype(bf16)
+    own_sums = jnp.sum(right_factor * right_factor, axis=1)[None]
+    last_left, own_sums = lax.optimization_barrier((left_factor, own_sums))
+    square_sums = jnp.sum(from_everyone(own_sums, TENSOR), axis=(0, 1))
+    orthonormal = (product(last_left, high, 1, 1) + product(last_left, low, 1, 1)).astype(bf16)
     inverse = lax.rsqrt(square_sums + epsilon)[:, None]
     full_factor = right_factor * inverse
     own_factor = lax.dynamic_slice_in_dim(full_factor, (z_hi * 4 + y) * columns, columns, 0).T

time: 209 us -> 185 us (0.89)
  waiting for transfers between devices: 54.6 us -> 37.4 us
  starting transfers between devices: 58.1 us -> 52.2 us
  matrix products: 21.8 us -> 17.1 us
  local copies, waits for them, and re-layouts: 4.83 us -> 8.1 us
    ppermute x14 -> x11, waiting for transfers between devices: 41.9 us -> 15.1 us  [from_ahead(): lax.ppermute(value, axis, [(i, (i - steps) % length) for i in range(lengt...]
    all_to_all x3 -> x4, waiting for transfers between devices: 12.7 us -> 22.4 us  [from_everyone(): lax.all_to_all(jnp.broadcast_to(value[None], (length, *value.shape)), axi...]
    ppermute x14 -> x11, starting transfers between devices: 32.5 us -> 23.5 us  [from_ahead(): lax.ppermute(value, axis, [(i, (i - steps) % length) for i in range(lengt...]
    all_to_all x3 -> x4, starting transfers between devices: 19 us -> 25.1 us  [from_everyone(): lax.all_to_all(jnp.broadcast_to(value[None], (length, *value.shape)), axi...]
    dot_general x10, matrix products: 21.8 us -> 17.1 us  [product(): lax.dot_general(left, right, (((left_dim,), (right_dim,)), ((), ())), pre...]
    all_to_all x1, starting transfers between devices: 6.67 us -> 3.51 us  [on_device(): lax.all_to_all(partial_right.reshape(4, R // 4, -1), 'y', 0, 0, tiled=True)]
    unnamed x19 -> x33, local copies, waits for them, and re-layouts: 1.05 us -> 3.75 us
    pallas_call x1 -> x2, Pallas kernels: 18.3 us -> 18.6 us  [block_call(): pl.pallas_call(kernel, out_shape=[jax.ShapeDtypeStruct(shape, dtype) for...]
  transfers between devices with their start and end apart: 18 -> 16, of which waited for: 12 -> 11; matrix products, arithmetic and copies ran while one was open for 6% -> 5% of each run, Pallas kernels for 9% -> 10%
where the time goes in v1:
time: 185 us; the launch traced here: 184 us
  starting transfers between devices  52.2 us (28%)
  blocking collectives  43 us (23%)
  waiting for transfers between devices  37.4 us (20%)
  Pallas kernels  18.6 us (10%)
  matrix products  17.1 us (9%)
  local copies, waits for them, and re-layouts  8.1 us (4%)
  other arithmetic  6.86 us (4%)
    all_to_all x4, starting transfers between devices, from_everyone(): lax.all_to_all(jnp.broadcast_to(value[None], (length, *value.shape)), axi...  25.1 us
    ppermute x11, starting transfers between devices, from_ahead(): lax.ppermute(value, axis, [(i, (i - steps) % length) for i in range(lengt...  23.5 us
    all_to_all x1, blocking collectives, on_device(): lax.all_to_all(partial_left.reshape(FAR, -1, R), ('x', 'z_lo'), 0, 0, til...  23.4 us
    all_to_all x4, waiting for transfers between devices, from_everyone(): lax.all_to_all(jnp.broadcast_to(value[None], (length, *value.shape)), axi...  22.4 us
    all_to_all x1, blocking collectives, from_everyone(): lax.all_to_all(jnp.broadcast_to(value[None], (length, *value.shape)), axi...  19.6 us
    pallas_call x2, Pallas kernels, block_call(): pl.pallas_call(kernel, out_shape=[jax.ShapeDtypeStruct(shape, dtype) for...  18.6 us
    dot_general x10, matrix products, product(): lax.dot_general(left, right, (((left_dim,), (right_dim,)), ((), ())), pre...  17.1 us
    ppermute x11, waiting for transfers between devices, from_ahead(): lax.ppermute(value, axis, [(i, (i - steps) % length) for i in range(lengt...  15.1 us
  transfers between devices with their start and end apart: 16, of which 11 were waited for; matrix products, arithmetic and copies ran while one was open for 5% of the time, Pallas kernels for 10%

profile of v1, /device:TPU:1, one launch (start us, length us, event | category | flops | bytes accessed | tf_op | source)
XLA Modules:
  0.0 184.2 jit_solution(12606171082910393623)
XLA Ops:
  0.6 1.0 convert_bitcast_fusion
  1.6 7.8 %collective-permute-start = (bf16[64,896]{1,0:T(8,128)(2,1)S(1)}, bf16[64,896]{1,0:T(8,128)(2,1)S(1)}, u32[]{:S(2)}, u32[]{:S(2)}) collective-permute-start(bf16[64,896]{1,0:T(8,128)(2,1)S(1)} %convert_bitcast_fusion), channel_id=1, source_target_pairs={{0,128},{128,0},{1,129},{129,1},{2,130},{130,2},{3,131},{131,3},{4... | collective-permute-start | bytes 344072 | tf_op jit(solution)/shard_map/ppermute | solution.py:184
  9.4 2.3 %collective-permute-done = bf16[64,896]{1,0:T(8,128)(2,1)S(1)} collective-permute-done((bf16[64,896]{1,0:T(8,128)(2,1)S(1)}, bf16[64,896]{1,0:T(8,128)(2,1)S(1)}, u32[]{:S(2)}, u32[]{:S(2)}) %collective-permute-start) | collective-permute-done | bytes 114720 | tf_op jit(solution)/shard_map/ppermute | solution.py:184
  11.7 1.0 select_bitcast_fusion.1
  12.7 1.0 broadcast_in_dim.14
  13.8 4.8 %all-to-all-start = ((bf16[4,2,64,896]{3,2,1,0:T(8,128)(2,1)}), bf16[4,2,64,896]{3,2,1,0:T(8,128)(2,1)S(1)}, u32[]{:S(2)}, u32[]{:S(2)}) async-start(bf16[4,2,64,896]{3,2,1,0:T(8,128)(2,1)} %broadcast_in_dim.14), calls=%async_computation | async-start | bytes 1835008 | tf_op jit(solution)/shard_map/all_to_all | solution.py:179
  18.5 3.2 %add_convert_fusion = bf16[1024,896]{1,0:T(8,128)(2,1)} fusion(bf16[1024,896]{1,0:T(8,128)(2,1)S(1)} %copy-done.4, bf16[1024,896]{1,0:T(8,128)(2,1)} %param.3), kind=kLoop, calls=%fused_computation.2 | loop fusion | flops 3670016 | bytes 5505024 | tf_op jit(solution)/shard_map/convert_element_type | solution.py:204
  21.7 8.9 %all-to-all-done = bf16[4,2,64,896]{3,2,1,0:T(8,128)(2,1)S(1)} async-done(((bf16[4,2,64,896]{3,2,1,0:T(8,128)(2,1)}), bf16[4,2,64,896]{3,2,1,0:T(8,128)(2,1)S(1)}, u32[]{:S(2)}, u32[]{:S(2)}) %all-to-all-start) | async-done | bytes 917536 | tf_op jit(solution)/shard_map/all_to_all | solution.py:179
  30.7 0.9 copy-done.9
  31.7 0.7 convolution_convert_fusion.1
  32.4 2.6 %collective-permute-start.1 = (bf16[512,512]{1,0:T(8,128)(2,1)S(1)}, bf16[512,512]{1,0:T(8,128)(2,1)S(1)}, u32[]{:S(2)}, u32[]{:S(2)}) collective-permute-start(bf16[512,512]{1,0:T(8,128)(2,1)S(1)} %convolution_convert_fusion.1), channel_id=1, source_target_pairs={{0,1},{1,0},{2,3},{3,2},{4,5},{5,4},{6,7},{7,6},{8,9},{9,8},{10,11... | collective-permute-start | bytes 1572872 | tf_op jit(solution)/shard_map/ppermute | solution.py:184
  35.0 1.5 collective-permute-done.1
  36.6 1.9 %add_convert_fusion.2 = bf16[512,512]{1,0:T(8,128)(2,1)S(1)} fusion(bf16[512,512]{1,0:T(8,128)(2,1)S(1)} %collective-permute-done.1, bf16[512,896]{1,0:T(8,128)(2,1)} %bitcast.69, bf16[1024,896]{1,0:T(8,128)(2,1)S(1)} %copy-done.5, s32[]{:T(128)S(6)} %select_n.252), kind=kOutput, calls=%fused_computation.9 | convolution fusion | flops 470548480 | bytes 2883588 | tf_op jit(solution)/shard_map/dot_general | solution.py:29
  38.5 23.4 %all_to_all.35 = bf16[16,32,512]{2,1,0:T(8,128)(2,1)S(1)} all-to-all(bf16[16,32,512]{2,1,0:T(8,128)(2,1)S(1)} %bitcast.70), channel_id=1, replica_groups=mesh['z_hi'=2,'y'=4,'x'=4,'z_lo'=4,'core'=2] {'x','z_lo'}, dimensions={0} | all-to-all | bytes 1048576 | tf_op jit(solution)/shard_map/all_to_all | solution.py:212
  62.0 19.6 %all_to_all.36 = bf16[16,32,512]{2,1,0:T(8,128)(2,1)S(1)} all-to-all(bf16[16,32,512]{2,1,0:T(8,128)(2,1)S(1)} %broadcast_in_dim.15), channel_id=1, replica_groups=mesh['z_hi'=2,'y'=4,'x'=4,'z_lo'=4,'core'=2] {'x','z_lo'}, dimensions={0} | all-to-all | bytes 1048576 | tf_op jit(solution)/shard_map/all_to_all | solution.py:179
  81.7 1.7 collective-permute-start.2
  83.4 1.7 collective-permute-done.2
  85.0 1.1 broadcast_select_fusion.1
  86.2 0.7 fusion.9
  87.8 6.7 %all-to-all-start.3 = ((f32[8,40,128]{2,1,0:T(8,128)}), f32[8,40,128]{2,1,0:T(8,128)S(1)}, u32[]{:S(2)}, u32[]{:S(2)}) async-start(f32[8,40,128]{2,1,0:T(8,128)} %broadcast_in_dim.16), calls=%async_computation.3 | async-start | bytes 327680 | tf_op jit(solution)/shard_map/all_to_all | solution.py:179
  94.5 2.2 %convolution_convert_fusion = bf16[512,896]{1,0:T(8,128)(2,1)} fusion(bf16[1024,896]{1,0:T(8,128)(2,1)S(1)} %copy-done.5, bf16[512,512]{1,0:T(8,128)(2,1)S(1)} %get-tuple-element.36, bf16[512,512]{1,0:T(8,128)(2,1)S(1)} %get-tuple-element.35), kind=kOutput, calls=%fused_computation.6 | convolution fusion | flops 942080000 | bytes 3801088 | tf_op jit(solution)/shard_map/dot_general | solution.py:29
  96.7 7.3 %all-to-all-done.3 = f32[8,40,128]{2,1,0:T(8,128)S(1)} async-done(((f32[8,40,128]{2,1,0:T(8,128)}), f32[8,40,128]{2,1,0:T(8,128)S(1)}, u32[]{:S(2)}, u32[]{:S(2)}) %all-to-all-start.3) | async-done | bytes 163872 | tf_op jit(solution)/shard_map/all_to_all | solution.py:179
  104.1 1.7 collective-permute-start.4
  105.8 1.0 collective-permute-start.3
  106.8 1.9 %collective-permute-done.3 = f32[40,128]{1,0:T(8,128)S(1)} collective-permute-done((f32[40,128]{1,0:T(8,128)S(1)}, f32[40,128]{1,0:T(8,128)S(1)}, u32[]{:S(2)}, u32[]{:S(2)}) %collective-permute-start.3) | collective-permute-done | bytes 20512 | tf_op jit(solution)/shard_map/ppermute | solution.py:184
  108.7 0.8 collective-permute-start.6
  109.5 3.5 %all-to-all-start.4 = ((bf16[4,128,896]{2,1,0:T(8,128)(2,1)}), bf16[4,128,896]{2,1,0:T(8,128)(2,1)S(1)}, u32[]{:S(2)}, u32[]{:S(2)}) async-start(bf16[4,128,896]{2,1,0:T(8,128)(2,1)} %bitcast.67), calls=%async_computation.4 | async-start | bytes 1835008 | tf_op jit(solution)/shard_map/all_to_all | solution.py:227
  113.0 0.9 collective-permute-start.8
  113.9 1.2 collective-permute-start.7
  115.1 4.7 %collective-permute-done.7 = f32[160,128]{1,0:T(8,128)S(1)} collective-permute-done((f32[160,128]{1,0:T(8,128)S(1)}, f32[160,128]{1,0:T(8,128)S(1)}, u32[]{:S(2)}, u32[]{:S(2)}) %collective-permute-start.7) | collective-permute-done | bytes 81952 | tf_op jit(solution)/shard_map/ppermute | solution.py:184
  119.9 5.1 %collective-permute-start.9 = (f32[640,128]{1,0:T(8,128)S(1)}, f32[640,128]{1,0:T(8,128)S(1)}, u32[]{:S(2)}, u32[]{:S(2)}) collective-permute-start(f32[640,128]{1,0:T(8,128)S(1)} %constant_dynamic-update-slice_fusion.4.own_ref), channel_id=1, source_target_pairs={{0,1},{1,0},{2,3},{3,2},{4,5},{5,4},{6,7},{7,6},{8,9},{9,8},{10,11... | collective-permute-start | bytes 983048 | tf_op jit(solution)/shard_map/ppermute | solution.py:184
  124.9 1.3 collective-permute-done.9.other_ref
  127.1 9.9 %shard_map.58 = (f32[384,128]{1,0:T(8,128)S(1)}, f32[512,256]{1,0:T(8,128)S(1)}) custom-call(s32[32]{0:T(128)S(1)} %stack.143.place_ref, f32[640,128]{1,0:T(8,128)S(1)} %constant_dynamic-update-slice_fusion.4.own_ref, f32[640,128]{1,0:T(8,128)S(1)} %collective-permute-done.9.other_ref), custom_call_target="tpu_custom_call" | custom-call | flops 1342177280 | bytes 2097152 | tf_op jit(solution)/shard_map/pallas_call | solution.py:166
  136.9 1.7 collective-permute-done.10
  138.7 1.0 broadcast_in_dim.17
  139.7 5.6 %all-to-all-start.5 = ((bf16[4,128,896]{2,1,0:T(8,128)(2,1)}), bf16[4,128,896]{2,1,0:T(8,128)(2,1)}, u32[]{:S(2)}, u32[]{:S(2)}) async-start(bf16[4,128,896]{2,1,0:T(8,128)(2,1)} %broadcast_in_dim.17), calls=%async_computation.5 | async-start | bytes 1835008 | tf_op jit(solution)/shard_map/all_to_all | solution.py:179
  145.3 8.7 %shard_map.59 = (bf16[512,512]{1,0:T(8,128)(2,1)S(1)}, bf16[512,512]{1,0:T(8,128)(2,1)S(1)}) custom-call(f32[384,128]{1,0:T(8,128)S(1)} %get-tuple-element.28.rest_ref, f32[512,256]{1,0:T(8,128)S(1)} %get-tuple-element.29.begun_ref), custom_call_target="tpu_custom_call" | custom-call | flops 1342177280 | bytes 2097152 | tf_op jit(solution)/shard_map/pallas_call | solution.py:166
  154.0 4.0 %all-to-all-done.5 = bf16[4,128,896]{2,1,0:T(8,128)(2,1)} async-done(((bf16[4,128,896]{2,1,0:T(8,128)(2,1)}), bf16[4,128,896]{2,1,0:T(8,128)(2,1)}, u32[]{:S(2)}, u32[]{:S(2)}) %all-to-all-start.5) | async-done | bytes 917536 | tf_op jit(solution)/shard_map/all_to_all | solution.py:179
  158.0 1.9 %fusion.10 = f32[512,896]{1,0:T(8,128)S(1)} fusion(bf16[512,512]{1,0:T(8,128)(2,1)S(1)} %get-tuple-element.30, bf16[512,896]{1,0:T(8,128)(2,1)} %bitcast.41), kind=kOutput, calls=%fused_computation.49 | convolution fusion | flops 469762048 | bytes 3276800 | tf_op jit(solution)/shard_map/dot_general | solution.py:29
  159.9 3.2 %multiply_reduce_fusion = (f32[512]{0:T(512)S(1)}, f32[512,896]{1,0:T(8,128)}) fusion(f32[512,896]{1,0:T(8,128)S(1)} %fusion.10, bf16[512,512]{1,0:T(8,128)(2,1)S(1)} %get-tuple-element.32, bf16[512,896]{1,0:T(8,128)(2,1)} %bitcast.41), kind=kOutput, calls=%fused_computation.4 | convolution fusion | flops 471137792 | bytes 5113856 | tf_op jit(solution)/shard_map/dot_general | solution.py:29
  163.8 8.1 %all-to-all-start.6 = ((f32[32,1,512]{2,1,0:T(1,128)}), f32[32,1,512]{2,1,0:T(1,128)S(1)}, u32[]{:S(2)}, u32[]{:S(2)}) async-start(f32[32,1,512]{2,1,0:T(1,128)} %broadcast_in_dim.20), calls=%async_computation.6 | async-start | bytes 131072 | tf_op jit(solution)/shard_map/all_to_all | solution.py:179
  171.9 0.7 fusion.11
  172.7 0.7 add_convert_fusion.1
  173.4 1.0 copy-done.7
  175.1 2.5 %subtract_convert_fusion = bf16[1024,896]{1,0:T(8,128)(2,1)} fusion(bf16[1024,896]{1,0:T(8,128)(2,1)S(1)} %copy-done.6, bf16[1024,512]{1,0:T(8,128)(2,1)S(1)} %add_convert_fusion.1, f32[512,896]{1,0:T(8,128)S(1)} %copy-done), kind=kOutput, calls=%fused_computation.1 | convolution fusion | flops 943652864 | bytes 6553600 | tf_op jit(solution)/shard_map/dot_general | solution.py:29
  177.6 2.1 %all-to-all-done.6 = f32[32,1,512]{2,1,0:T(1,128)S(1)} async-done(((f32[32,1,512]{2,1,0:T(1,128)}), f32[32,1,512]{2,1,0:T(1,128)S(1)}, u32[]{:S(2)}, u32[]{:S(2)}) %all-to-all-start.6) | async-done | bytes 65568 | tf_op jit(solution)/shard_map/all_to_all | solution.py:179
  180.0 1.0 copy-done.8
  181.0 2.5 %multiply_convert_fusion = bf16[1024,896]{1,0:T(8,128)(2,1)} fusion(bf16[1024,512]{1,0:T(8,128)(2,1)S(1)} %copy-done.8, f32[512,896]{1,0:T(8,128)S(1)} %broadcast_multiply_fusion), kind=kOutput, calls=%fused_computation | convolution fusion | flops 941817856 | bytes 4718592 | tf_op jit(solution)/shard_map/dot_general | solution.py:29
  (56 shorter events, 4.5 us)
Async XLA Ops:
  1.6 10.1 %collective-permute-start = (bf16[64,896]{1,0:T(8,128)(2,1)S(1)}, bf16[64,896]{1,0:T(8,128)(2,1)S(1)}, u32[]{:S(2)}, u32[]{:S(2)}) collective-permute-start(bf16[64,896]{1,0:T(8,128)(2,1)S(1)} %convert_bitcast_fusion), channel_id=1, source_target_pairs={{0,128},{128,0},{1,129},{129,1},{2,130},{130,2},{3,131},{131,3},{4... | collective-permute-start | bytes 344072 | tf_op jit(solution)/shard_map/ppermute | solution.py:184
  12.7 5.9 %copy-start.4 = (bf16[1024,896]{1,0:T(8,128)(2,1)S(1)}, bf16[1024,896]{1,0:T(8,128)(2,1)}, u32[]{:S(2)}) copy-start(bf16[1024,896]{1,0:T(8,128)(2,1)} %param.4) | copy-start | bytes 5505028
  13.8 16.9 %all-to-all-start = ((bf16[4,2,64,896]{3,2,1,0:T(8,128)(2,1)}), bf16[4,2,64,896]{3,2,1,0:T(8,128)(2,1)S(1)}, u32[]{:S(2)}, u32[]{:S(2)}) async-start(bf16[4,2,64,896]{3,2,1,0:T(8,128)(2,1)} %broadcast_in_dim.14), calls=%async_computation | async-start | bytes 1835008 | tf_op jit(solution)/shard_map/all_to_all | solution.py:179
  21.7 9.9 %copy-start.5 = (bf16[1024,896]{1,0:T(8,128)(2,1)S(1)}, bf16[1024,896]{1,0:T(8,128)(2,1)}, u32[]{:S(2)}) copy-start(bf16[1024,896]{1,0:T(8,128)(2,1)} %add_convert_fusion) | copy-start | bytes 5505028
  30.7 0.9 copy-start.9
  32.4 4.2 %collective-permute-start.1 = (bf16[512,512]{1,0:T(8,128)(2,1)S(1)}, bf16[512,512]{1,0:T(8,128)(2,1)S(1)}, u32[]{:S(2)}, u32[]{:S(2)}) collective-permute-start(bf16[512,512]{1,0:T(8,128)(2,1)S(1)} %convolution_convert_fusion.1), channel_id=1, source_target_pairs={{0,1},{1,0},{2,3},{3,2},{4,5},{5,4},{6,7},{7,6},{8,9},{9,8},{10,11... | collective-permute-start | bytes 1572872 | tf_op jit(solution)/shard_map/ppermute | solution.py:184
  81.7 3.4 %collective-permute-start.2 = (bf16[512,512]{1,0:T(8,128)(2,1)S(1)}, bf16[512,512]{1,0:T(8,128)(2,1)}, u32[]{:S(2)}, u32[]{:S(2)}) collective-permute-start(bf16[512,512]{1,0:T(8,128)(2,1)S(1)} %bitcast.66), channel_id=1, source_target_pairs={{0,1},{1,0},{2,3},{3,2},{4,5},{5,4},{6,7},{7,6},{8,9},{9,8},{10,11... | collective-permute-start | bytes 1572872 | tf_op jit(solution)/shard_map/ppermute | solution.py:184
  86.2 8.3 %copy-start.2 = (bf16[512,512]{1,0:T(8,128)(2,1)}, bf16[512,512]{1,0:T(8,128)(2,1)S(1)}, u32[]{:S(2)}) copy-start(bf16[512,512]{1,0:T(8,128)(2,1)S(1)} %get-tuple-element.36) | copy-start | bytes 1572868
  87.8 16.2 %all-to-all-start.3 = ((f32[8,40,128]{2,1,0:T(8,128)}), f32[8,40,128]{2,1,0:T(8,128)S(1)}, u32[]{:S(2)}, u32[]{:S(2)}) async-start(f32[8,40,128]{2,1,0:T(8,128)} %broadcast_in_dim.16), calls=%async_computation.3 | async-start | bytes 327680 | tf_op jit(solution)/shard_map/all_to_all | solution.py:179
  104.0 4.7 %collective-permute-start.5 = (f32[40,128]{1,0:T(8,128)S(1)}, f32[40,128]{1,0:T(8,128)S(1)}, u32[]{:S(2)}, u32[]{:S(2)}) collective-permute-start(f32[40,128]{1,0:T(8,128)S(1)} %reduce_sum.52), channel_id=1, source_target_pairs={{0,8},{8,16},{16,24},{24,0},{1,9},{9,17},{17,25},{25,1},{2,10},{10... | collective-permute-start | bytes 61448 | tf_op jit(solution)/shard_map/ppermute | solution.py:184
  104.1 4.6 %collective-permute-start.4 = (f32[40,128]{1,0:T(8,128)S(1)}, f32[40,128]{1,0:T(8,128)S(1)}, u32[]{:S(2)}, u32[]{:S(2)}) collective-permute-start(f32[40,128]{1,0:T(8,128)S(1)} %reduce_sum.52), channel_id=1, source_target_pairs={{0,16},{8,24},{16,0},{24,8},{1,17},{9,25},{17,1},{25,9},{2,18},{10... | collective-permute-start | bytes 61448 | tf_op jit(solution)/shard_map/ppermute | solution.py:184
  105.8 2.9 %collective-permute-start.3 = (f32[40,128]{1,0:T(8,128)S(1)}, f32[40,128]{1,0:T(8,128)S(1)}, u32[]{:S(2)}, u32[]{:S(2)}) collective-permute-start(f32[40,128]{1,0:T(8,128)S(1)} %reduce_sum.52), channel_id=1, source_target_pairs={{0,24},{8,0},{16,8},{24,16},{1,25},{9,1},{17,9},{25,17},{2,26},{10... | collective-permute-start | bytes 61448 | tf_op jit(solution)/shard_map/ppermute | solution.py:184
  108.7 6.3 %collective-permute-start.6 = (f32[160,128]{1,0:T(8,128)S(1)}, f32[160,128]{1,0:T(8,128)S(1)}, u32[]{:S(2)}, u32[]{:S(2)}) collective-permute-start(f32[160,128]{1,0:T(8,128)S(1)} %get-tuple-element.39), channel_id=1, source_target_pairs={{0,6},{2,0},{4,2},{6,4},{1,7},{3,1},{5,3},{7,5},{8,14},{10,8},{12,... | collective-permute-start | bytes 245768 | tf_op jit(solution)/shard_map/ppermute | solution.py:184
  109.5 16.7 %all-to-all-start.4 = ((bf16[4,128,896]{2,1,0:T(8,128)(2,1)}), bf16[4,128,896]{2,1,0:T(8,128)(2,1)S(1)}, u32[]{:S(2)}, u32[]{:S(2)}) async-start(bf16[4,128,896]{2,1,0:T(8,128)(2,1)} %bitcast.67), calls=%async_computation.4 | async-start | bytes 1835008 | tf_op jit(solution)/shard_map/all_to_all | solution.py:227
  113.0 6.8 %collective-permute-start.8 = (f32[160,128]{1,0:T(8,128)S(1)}, f32[160,128]{1,0:T(8,128)S(1)}, u32[]{:S(2)}, u32[]{:S(2)}) collective-permute-start(f32[160,128]{1,0:T(8,128)S(1)} %get-tuple-element.39), channel_id=1, source_target_pairs={{0,2},{2,4},{4,6},{6,0},{1,3},{3,5},{5,7},{7,1},{8,10},{10,12},{12... | collective-permute-start | bytes 245768 | tf_op jit(solution)/shard_map/ppermute | solution.py:184
  113.9 5.9 %collective-permute-start.7 = (f32[160,128]{1,0:T(8,128)S(1)}, f32[160,128]{1,0:T(8,128)S(1)}, u32[]{:S(2)}, u32[]{:S(2)}) collective-permute-start(f32[160,128]{1,0:T(8,128)S(1)} %get-tuple-element.39), channel_id=1, source_target_pairs={{0,4},{2,6},{4,0},{6,2},{1,5},{3,7},{5,1},{7,3},{8,12},{10,14},{12... | collective-permute-start | bytes 245768 | tf_op jit(solution)/shard_map/ppermute | solution.py:184
  119.9 6.3 %collective-permute-start.9 = (f32[640,128]{1,0:T(8,128)S(1)}, f32[640,128]{1,0:T(8,128)S(1)}, u32[]{:S(2)}, u32[]{:S(2)}) collective-permute-start(f32[640,128]{1,0:T(8,128)S(1)} %constant_dynamic-update-slice_fusion.4.own_ref), channel_id=1, source_target_pairs={{0,1},{1,0},{2,3},{3,2},{4,5},{5,4},{6,7},{7,6},{8,9},{9,8},{10,11... | collective-permute-start | bytes 983048 | tf_op jit(solution)/shard_map/ppermute | solution.py:184
  126.3 12.3 %collective-permute-start.10 = (bf16[128,896]{1,0:T(8,128)(2,1)S(1)}, bf16[128,896]{1,0:T(8,128)(2,1)S(1)}, u32[]{:S(2)}, u32[]{:S(2)}) collective-permute-start(bf16[128,896]{1,0:T(8,128)(2,1)S(1)} %reduce_sum.53), channel_id=1, source_target_pairs={{0,128},{128,0},{1,129},{129,1},{2,130},{130,2},{3,131},{131,3},{4... | collective-permute-start | bytes 688136 | tf_op jit(solution)/shard_map/ppermute | solution.py:184
  138.6 6.6 %copy-start.3 = (bf16[512,512]{1,0:T(8,128)(2,1)S(1)}, bf16[512,512]{1,0:T(8,128)(2,1)}, u32[]{:S(2)}) copy-start(bf16[512,512]{1,0:T(8,128)(2,1)} %copy-done.2) | copy-start | bytes 1572868
  139.7 18.4 %all-to-all-start.5 = ((bf16[4,128,896]{2,1,0:T(8,128)(2,1)}), bf16[4,128,896]{2,1,0:T(8,128)(2,1)}, u32[]{:S(2)}, u32[]{:S(2)}) async-start(bf16[4,128,896]{2,1,0:T(8,128)(2,1)} %broadcast_in_dim.17), calls=%async_computation.5 | async-start | bytes 1835008 | tf_op jit(solution)/shard_map/all_to_all | solution.py:179
  163.8 15.9 %all-to-all-start.6 = ((f32[32,1,512]{2,1,0:T(1,128)}), f32[32,1,512]{2,1,0:T(1,128)S(1)}, u32[]{:S(2)}, u32[]{:S(2)}) async-start(f32[32,1,512]{2,1,0:T(1,128)} %broadcast_in_dim.20), calls=%async_computation.6 | async-start | bytes 131072 | tf_op jit(solution)/shard_map/all_to_all | solution.py:179
  172.6 1.8 copy-start
  172.7 2.4 %copy-start.6 = (bf16[1024,896]{1,0:T(8,128)(2,1)S(1)}, bf16[1024,896]{1,0:T(8,128)(2,1)}, u32[]{:S(2)}) copy-start(bf16[1024,896]{1,0:T(8,128)(2,1)} %add_convert_fusion) | copy-start | bytes 5505028
  173.4 1.0 copy-start.7
  175.1 4.7 %copy-start.1 = (f32[512,896]{1,0:T(8,128)S(1)}, f32[512,896]{1,0:T(8,128)}, u32[]{:S(2)}) copy-start(f32[512,896]{1,0:T(8,128)} %get-tuple-element.48) | copy-start | bytes 5505028
  179.8 1.2 copy-start.8
